TPU v7x, 256 devices: a whole 4x4x8 slice. The times are simulated.
256 devices in a mesh: row: 16 (over y_hi, z), col: 16 (over x, y_lo, core).
Axes of the slice: x: 4, y: 4 (y_hi: 2, y_lo: 2; y = y_hi * 2 + y_lo), z: 8, core: 2. Of those that a mesh axis runs over, the one named last changes fastest.
Arguments:
- amplitudes: bfloat16 [49152, 12288], P('row', 'col'), may hold values from -6 to 6
- pair_mask: int32 [192, 48], P('row', 'col'), may hold values 0 or 1
- integrals: bfloat16 [16, 16, 2, 256, 256], P('row', 'col'), may hold values from -0.25 to 0.25
- tile_list: int32 [16, 16, 2], P('row', 'col'), may hold values from 0 to 2, as said below
- tile_count: int32 [16, 16], P('row', 'col'), may hold values from 1 to 2, as said below
- owner: int32 [4, 16], P(None, 'col'), may hold values from 0 to 15, as said below
Outputs:
- ladder: bfloat16 [49152, 4096], P('row', 'col')
Inputs may be any that keep to these rules, and one draw needn't show every extreme that they name: `owner`: within a column the 4 owners differ. `tile_count`: some panel that serves a step has all 2 slots live. `tile_list`: the live slots of a panel name distinct cd tile pairs; entries past the count are in range and unused.
All inputs are finite; a program needn't handle non-finite values. No bound on the sum of `pair_mask` on one device may be relied on, other than what follows from the above.
Results may differ from a plain program's by a relative error of at most 0.001.
Values may be sent and summed in bfloat16 or wider, within the bound.
A program may use at most 128 MiB of HBM per device.

v0:
```python
import jax
import jax.numpy as jnp
from jax import lax
from jax.sharding import PartitionSpec as P

STEPS = 4


def passed_along(value, axis, by):
    peers = lax.axis_size(axis)
    return lax.ppermute(value, axis, [(i, (i + by) % peers) for i in range(peers)])


def broadcast(value, axis, source):
    kept = jnp.where(lax.axis_index(axis) == source, value, 0).astype(value.dtype)
    return lax.psum(kept, axis)


def slot_product(current, panel_tiles, slot_tiles, slot_index, tile_width):
    start = slot_tiles[slot_index] * tile_width
    tile_block = lax.dynamic_slice_in_dim(current, start, tile_width, 1)
    weights = lax.dynamic_index_in_dim(panel_tiles, slot_index, 0, keepdims=False)
    return jnp.dot(tile_block, weights, preferred_element_type=jnp.float32)


def shards(amplitudes, pair_mask, integrals, tile_list, tile_count, owner):
    row_count, full_width = amplitudes.shape
    tile_width = integrals.shape[-1]
    block_count, local_tiles = pair_mask.shape
    slot_total = integrals.shape[2]
    shaped = amplitudes.reshape(block_count, row_count // block_count, local_tiles, tile_width)
    masked = (shaped * pair_mask.astype(jnp.bfloat16)[:, None, :, None]).reshape(
        row_count, full_width
    )
    running = jnp.zeros((row_count, tile_width), jnp.float32)
    current = masked
    for grid_step in range(STEPS):
        if grid_step > 0:
            current = passed_along(current, "col", 1)
        panel_tiles, slot_tiles, live_count = (
            broadcast(integrals[0, 0], "row", owner[grid_step, 0]),
            broadcast(tile_list[0, 0], "row", owner[grid_step, 0]),
            broadcast(tile_count[0, 0], "row", owner[grid_step, 0]),
        )
        for slot_index in range(slot_total):
            product = slot_product(current, panel_tiles, slot_tiles, slot_index, tile_width)
            running = running + jnp.where(slot_index < live_count, product, jnp.zeros_like(product))
    return running.astype(jnp.bfloat16)


def solution(mesh):
    return jax.shard_map(
        shards,
        mesh=mesh,
        in_specs=(
            P("row", "col"),
            P("row", "col"),
            P("row", "col", None, None, None),
            P("row", "col", None),
            P("row", "col"),
            P(None, "col"),
        ),
        out_specs=P("row", "col"),
        check_vma=False,
    )
```

profile of v0, /device:TPU:2, one launch (start us, length us, event | category | flops | bytes accessed | tf_op | source)
XLA Modules:
  0.0 333.6 jit_solution(6793563908620637323)
XLA Ops:
  6.5 0.0 all-reduce.4.cloned.1.call-start
  6.5 0.7 convert_element_type.11
  7.2 0.5 mul.59
  7.7 5.3 %copy.9 = bf16[96,8,12,256]{3,1,2,0:T(8,128)(2,1)} copy(bf16[96,8,12,256]{3,2,1,0:T(8,128)(2,1)S(1)} %bitcast.62) | data formatting | bytes 9437184
  13.0 6.6 %copy.8 = bf16[3072,768]{0,1:T(8,128)(2,1)} copy(bf16[3072,768]{1,0:T(8,128)(2,1)} %param.6) | data formatting | bytes 9437184 | tf_op args[0]
  19.7 0.0 copy-start.7
  19.7 0.0 copy-start.2
  19.7 0.0 copy-start.8
  19.7 5.7 %mul.61 = bf16[3072,768]{0,1:T(8,128)(2,1)S(1)} multiply(bf16[3072,768]{0,1:T(8,128)(2,1)} %copy.8, bf16[3072,768]{0,1:T(8,128)(2,1)} %bitcast.63) | non-fusion elementwise | flops 2359296 | bytes 14155776 | tf_op jit(solution)/shard_map/mul | solution.py:32
  25.4 0.0 copy-start
  25.4 2.1 copy-done
  27.5 0.0 collective-permute-start
  27.5 54.4 %collective-permute-done = bf16[3072,768]{0,1:T(8,128)(2,1)S(1)} collective-permute-done((bf16[3072,768]{0,1:T(8,128)(2,1)S(1)}, bf16[3072,768]{0,1:T(8,128)(2,1)S(1)}, u32[]{:S(2)}, u32[]{:S(2)}) %collective-permute-start) | collective-permute-done | bytes 4718624 | tf_op jit(solution)/shard_map/ppermute | solution.py:11
  82.0 0.0 copy-start.1
  82.0 2.2 copy-done.1
  84.2 0.0 collective-permute-start.1
  84.2 54.5 %collective-permute-done.1 = bf16[3072,768]{0,1:T(8,128)(2,1)} collective-permute-done((bf16[3072,768]{0,1:T(8,128)(2,1)S(1)}, bf16[3072,768]{0,1:T(8,128)(2,1)}, u32[]{:S(2)}, u32[]{:S(2)}) %collective-permute-start.1) | collective-permute-done | bytes 4718624 | tf_op jit(solution)/shard_map/ppermute | solution.py:11
  138.8 0.0 collective-permute-start.2
  138.8 0.0 copy-done.7
  138.8 0.7 fusion.32
  142.0 0.0 copy-done.2
  142.1 1.0 select_bitcast_fusion.3
  143.0 0.0 all-reduce.4.cloned.1.call-update
  143.7 0.0 copy-done.8
  143.8 21.6 %all-reduce = (s32[2]{0:T(128)S(1)}, s32[]{:T(128)}, s32[2]{0:T(128)S(1)}, s32[]{:T(128)}, s32[2]{0:T(128)S(1)}, /*index=5*/s32[]{:T(128)}, s32[2]{0:T(128)S(1)}, s32[]{:T(128)}) all-reduce(s32[2]{0:T(128)S(1)} %get-tuple-element.31, s32[]{:T(128)S(6)} %select_n.211, ...), channel_id=1, replica_groups=mesh['row'=16,'col'=16] {'row'}, use_global_device_ids=true, to_apply=%region_10.11 | all-reduce | flops 12 | bytes 96 | tf_op jit(solution)/shard_map/psum | solution.py:16
  165.3 0.7 fusion.30
  171.1 0.7 fusion.28
  176.9 134.2 %all-reduce.4.cloned.1.call-done = (bf16[2,256,256]{2,1,0:T(8,128)(2,1)}, bf16[2,256,256]{2,1,0:T(8,128)(2,1)}, bf16[2,256,256]{2,1,0:T(8,128)(2,1)}, bf16[2,256,256]{2,1,0:T(8,128)(2,1)}) async-done(((bf16[2,256,256]{2,1,0:T(8,128)(2,1)}, bf16[2,256,256]{2,1,0:T(8,128)(2,1)}, bf16[2,256,256]{2,1,0:T(8,128)(2,1)}, bf16[2,256,256]{2,1,0:T(8,128)(2,1)}), (bf16[2,256,256]{2,1,0:T(8,128)(2,1)}, ...) | async-done | bytes 1048592 | tf_op jit(solution)/shard_map/psum | solution.py:16
  311.1 0.0 copy-start.6
  311.1 0.0 slice-start
  311.1 2.2 convolution_select_fusion.6
  313.2 0.0 copy-done.6
  313.3 0.0 slice-start.1
  313.3 0.0 copy-start.5
  313.3 2.2 fusion
  315.5 0.0 slice-done
  315.5 0.0 slice-done.1
  315.5 0.0 copy-done.5
  315.5 0.6 convolution_select_fusion.4
  316.1 0.0 copy-start.4
  316.1 0.7 fusion.2
  316.8 0.3 copy-done.4
  317.1 2.0 convolution_select_fusion.2
  319.1 0.0 copy-start.3
  319.1 2.2 fusion.4
  321.3 0.0 collective-permute-done.2
  321.4 0.0 copy-done.3
  321.4 2.0 convolution_select_fusion
  323.4 3.4 %fusion.7 = bf16[3072,256]{1,0:T(8,128)(2,1)} fusion(f32[3072,256]{1,0:T(8,128)S(1)} %convolution_select_fusion, f32[3072,256]{1,0:T(8,128)S(1)} %fusion.4, bf16[3072,768]{0,1:T(8,128)(2,1)} %collective-permute-done.2, s32[]{:T(128)S(6)} %select_n.216, pred[]{:T(512)S(6)} %gt.30, bf16[2,256,256]{2,1,0:T(8,128)(2,1)S(1)} %copy-done.3), kind=kOutput, calls=%fused_computation.15 | convolution fusion | flops 405798912 | bytes 9568261 | tf_op jit(solution)/shard_map/dot_general | solution.py:23
  (2 shorter events, 0.0 us)
Async XLA Ops:
  6.5 304.5 %all-reduce.4.cloned.1.call-start = ((), (), s32[]{:S(2)}) async-start(), calls=%async_computation | async-start | bytes 2097152 | tf_op jit(solution)/shard_map/psum | solution.py:16
  19.7 119.1 %copy-start.7 = (s32[4,1]{0,1:T(1,128)S(1)}, s32[4,1]{0,1:T(1,128)}, u32[]{:S(2)}) copy-start(s32[4,1]{0,1:T(1,128)} %param.11) | copy-start | bytes 52
  19.7 122.4 %copy-start.2 = (bf16[1,1,2,256,256]{4,3,2,1,0:T(8,128)(2,1)S(1)}, bf16[1,1,2,256,256]{4,3,2,1,0:T(8,128)(2,1)}, u32[]{:S(2)}) copy-start(bf16[1,1,2,256,256]{4,3,2,1,0:T(8,128)(2,1)} %param.8) | copy-start | bytes 786436
  19.7 124.1 %copy-start.8 = (s32[1,1,2]{2,1,0:T(1,128)S(1)}, s32[1,1,2]{2,1,0:T(1,128)}, u32[]{:S(2)}) copy-start(s32[1,1,2]{2,1,0:T(1,128)} %param.9) | copy-start | bytes 28
  25.4 2.1 copy-start
  27.5 54.4 %collective-permute-start = (bf16[3072,768]{0,1:T(8,128)(2,1)S(1)}, bf16[3072,768]{0,1:T(8,128)(2,1)S(1)}, u32[]{:S(2)}, u32[]{:S(2)}) collective-permute-start(bf16[3072,768]{0,1:T(8,128)(2,1)S(1)} %mul.61), channel_id=1, source_target_pairs={{0,1},{1,2},{2,3},{3,4},{4,5},{5,6},{6,7},{7,8},{8,9},{9,10},{10,1... | collective-permute-start | bytes 14155784 | tf_op jit(solution)/shard_map/ppermute | solution.py:11
  82.0 2.2 copy-start.1
  84.2 54.6 %collective-permute-start.1 = (bf16[3072,768]{0,1:T(8,128)(2,1)S(1)}, bf16[3072,768]{0,1:T(8,128)(2,1)}, u32[]{:S(2)}, u32[]{:S(2)}) collective-permute-start(bf16[3072,768]{0,1:T(8,128)(2,1)S(1)} %collective-permute-done), channel_id=1, source_target_pairs={{0,1},{1,2},{2,3},{3,4},{4,5},{5,6},{6,7},{7,8},{8,9},{9,10},{10,1... | collective-permute-start | bytes 14155784 | tf_op jit(solution)/shard_map/ppermute | solution.py:11
  138.8 182.6 %collective-permute-start.2 = (bf16[3072,768]{0,1:T(8,128)(2,1)}, bf16[3072,768]{0,1:T(8,128)(2,1)}, u32[]{:S(2)}, u32[]{:S(2)}) collective-permute-start(bf16[3072,768]{0,1:T(8,128)(2,1)} %collective-permute-done.1), channel_id=1, source_target_pairs={{0,1},{1,2},{2,3},{3,4},{4,5},{5,6},{6,7},{7,8},{8,9},{9,10},{10,1... | collective-permute-start | bytes 14155784 | tf_op jit(solution)/shard_map/ppermute | solution.py:11
  311.1 2.2 copy-start.6
  311.1 4.4 %slice-start = ((s8[4718592]{0:T(1024)(128)(4,1)}), s8[4194304]{0:T(1024)(128)(4,1)S(1)}, s32[]{:S(2)}) async-start(s8[4718592]{0:T(1024)(128)(4,1)} %bitcast.64), calls=%async_computation.1 | async-start | bytes 8388608
  313.3 2.2 slice-start.1
  313.3 2.2 copy-start.5
  316.1 1.0 copy-start.4
  319.1 2.2 copy-start.3
Sparse Core Ops, SparseCore 0:
  143.2 167.8 all-reduce.3
where the time goes:
time: 334 us
  waiting for transfers between devices  243 us (73%)
  between operations  27.1 us (8%)
  blocking collectives  21.6 us (6%)
  local copies, waits for them, and re-layouts  19.1 us (6%)
  matrix products  15.3 us (5%)
  other arithmetic  7.4 us (2%)
    psum x1, waiting for transfers between devices, broadcast(): return lax.psum(kept, axis)  134 us
    ppermute x3, waiting for transfers between devices, passed_along(): lax.ppermute(value, axis, [(i, (i + by) % peers) for i in range(peers)])  109 us
    psum x1, blocking collectives, broadcast(): return lax.psum(kept, axis)  21.6 us
    unnamed x24, local copies, waits for them, and re-layouts  16.6 us
    dot_general x8, matrix products, slot_product(): return jnp.dot(tile_block, weights, preferred_element_type=jnp.float32)  15.3 us
  transfers between devices with their start and end apart: 4, of which 3 were waited for; matrix products, arithmetic and copies ran while one was open for 4% of the time, Pallas kernels for 0%

commit v1 on v0

--- a/solution.py
+++ b/solution.py
@@ -13,7 +13,7 @@
 
 def broadcast(value, axis, source):
     kept = jnp.where(lax.axis_index(axis) == source, value, 0).astype(value.dtype)
-    return lax.psum(kept, axis)
+    return jnp.sum(lax.all_gather(kept, axis), axis=0)
 
 
 def slot_product(current, panel_tiles, slot_tiles, slot_index, tile_width):

time: 334 us -> 566 us (1.69)
  blocking collectives: 21.6 us -> 170 us
  starting transfers between devices: 0.01 us -> 40.5 us
  waiting for transfers between devices: 243 us -> 265 us
  other arithmetic: 7.4 us -> 25 us
    all_gather x0 -> x4, waiting for transfers between devices: none -> 175 us  [broadcast(): return jnp.sum(lax.all_gather(kept, axis), axis=0)]
    all_gather x0 -> x4, blocking collectives: none -> 158 us  [broadcast(): return jnp.sum(lax.all_gather(kept, axis), axis=0)]
    psum x1 -> x0, waiting for transfers between devices: 134 us -> none  [broadcast(): return lax.psum(kept, axis)]
    ppermute x3, starting transfers between devices: 0.01 us -> 40.4 us  [passed_along(): lax.ppermute(value, axis, [(i, (i + by) % peers) for i in range(peers)])]
    psum x1 -> x0, blocking collectives: 21.6 us -> none  [broadcast(): return lax.psum(kept, axis)]
    ppermute x3, waiting for transfers between devices: 109 us -> 89 us  [passed_along(): lax.ppermute(value, axis, [(i, (i + by) % peers) for i in range(peers)])]
    reduce_sum x0 -> x12, other arithmetic: none -> 14.2 us  [broadcast(): return jnp.sum(lax.all_gather(kept, axis), axis=0)]
    unnamed x0 -> x1, blocking collectives: none -> 11.2 us
  transfers between devices with their start and end apart: 4 -> 7, of which waited for: 3 -> 4; matrix products, arithmetic and copies ran while one was open for 4% -> 10% of each run, Pallas kernels for 0% -> 0%
where the time goes in v1:
time: 566 us; the launch traced here: 565 us
  waiting for transfers between devices  265 us (47%)
  blocking collectives  170 us (30%)
  starting transfers between devices  40.5 us (7%)
  between operations  26.3 us (5%)
  other arithmetic  25 us (4%)
  local copies, waits for them, and re-layouts  20.2 us (4%)
  matrix products  17.9 us (3%)
    all_gather x4, waiting for transfers between devices, broadcast(): return jnp.sum(lax.all_gather(kept, axis), axis=0)  175 us
    all_gather x4, blocking collectives, broadcast(): return jnp.sum(lax.all_gather(kept, axis), axis=0)  158 us
    ppermute x3, waiting for transfers between devices, passed_along(): lax.ppermute(value, axis, [(i, (i + by) % peers) for i in range(peers)])  89 us
    ppermute x3, starting transfers between devices, passed_along(): lax.ppermute(value, axis, [(i, (i + by) % peers) for i in range(peers)])  40.4 us
    dot_general x8, matrix products, slot_product(): return jnp.dot(tile_block, weights, preferred_element_type=jnp.float32)  17.9 us
    unnamed x15, local copies, waits for them, and re-layouts  15.8 us
    reduce_sum x12, other arithmetic, broadcast(): return jnp.sum(lax.all_gather(kept, axis), axis=0)  14.2 us
  transfers between devices with their start and end apart: 7, of which 4 were waited for; matrix products, arithmetic and copies ran while one was open for 10% of the time, Pallas kernels for 0%

profile of v1, /device:TPU:2, one launch (start us, length us, event | category | flops | bytes accessed | tf_op | source)
XLA Modules:
  0.0 564.7 jit_solution(16149514658879257499)
XLA Ops:
  6.5 0.0 all-gather.13.cloned.1.call-start
  6.5 1.5 fusion.28
  10.5 2.0 broadcast_select_fusion.3
  12.5 0.0 all-gather.13.cloned.1.call-update
  12.5 0.0 all-gather.15.cloned.1.call-start
  12.6 0.7 all-gather.15.cloned.1.call-update
  13.3 0.0 all-gather.17.cloned.1.call-start
  13.3 0.7 all-gather.17.cloned.1.call-update
  14.0 0.0 all-gather.19.cloned.1.call-start
  14.1 0.7 convert_element_type.9
  14.8 0.5 mul.59
  15.2 5.3 copy.10
  20.5 6.7 %copy.9 = bf16[3072,768]{0,1:T(8,128)(2,1)} copy(bf16[3072,768]{1,0:T(8,128)(2,1)} %param.6) | data formatting | bytes 9437184 | tf_op args[0]
  27.2 0.0 copy-start
  27.2 0.0 copy-start.1
  27.2 8.1 %mul.61 = bf16[3072,768]{0,1:T(8,128)(2,1)} multiply(bf16[3072,768]{0,1:T(8,128)(2,1)} %copy.9, bf16[3072,768]{0,1:T(8,128)(2,1)} %bitcast.52) | non-fusion elementwise | flops 2359296 | bytes 14155776 | tf_op jit(solution)/shard_map/mul | solution.py:32
  35.3 0.0 collective-permute-start
  35.3 0.0 all-gather.19.cloned.1.call-update
  35.3 54.8 %collective-permute-done = bf16[3072,768]{0,1:T(8,128)(2,1)} collective-permute-done((bf16[3072,768]{0,1:T(8,128)(2,1)}, bf16[3072,768]{0,1:T(8,128)(2,1)}, u32[]{:S(2)}, u32[]{:S(2)}) %collective-permute-start) | collective-permute-done | bytes 4718624 | tf_op jit(solution)/shard_map/ppermute | solution.py:11
  90.1 20.7 %collective-permute-start.1 = (bf16[3072,768]{0,1:T(8,128)(2,1)}, bf16[3072,768]{0,1:T(8,128)(2,1)}, u32[]{:S(2)}, u32[]{:S(2)}) collective-permute-start(bf16[3072,768]{0,1:T(8,128)(2,1)} %collective-permute-done), channel_id=1, source_target_pairs={{0,1},{1,2},{2,3},{3,4},{4,5},{5,6},{6,7},{7,8},{8,9},{9,10},{10,1... | collective-permute-start | bytes 14155784 | tf_op jit(solution)/shard_map/ppermute | solution.py:11
  110.8 34.2 %collective-permute-done.1 = bf16[3072,768]{0,1:T(8,128)(2,1)} collective-permute-done((bf16[3072,768]{0,1:T(8,128)(2,1)}, bf16[3072,768]{0,1:T(8,128)(2,1)}, u32[]{:S(2)}, u32[]{:S(2)}) %collective-permute-start.1) | collective-permute-done | bytes 4718624 | tf_op jit(solution)/shard_map/ppermute | solution.py:11
  145.0 19.7 %collective-permute-start.2 = (bf16[3072,768]{0,1:T(8,128)(2,1)}, bf16[3072,768]{0,1:T(8,128)(2,1)}, u32[]{:S(2)}, u32[]{:S(2)}) collective-permute-start(bf16[3072,768]{0,1:T(8,128)(2,1)} %collective-permute-done.1), channel_id=1, source_target_pairs={{0,1},{1,2},{2,3},{3,4},{4,5},{5,6},{6,7},{7,8},{8,9},{9,10},{10,1... | collective-permute-start | bytes 14155784 | tf_op jit(solution)/shard_map/ppermute | solution.py:11
  164.7 0.0 copy-done
  164.7 43.6 %all-gather = s32[16,1,2]{2,1,0:T(1,128)S(1)} all-gather(s32[1,1,2]{2,1,0:T(1,128)S(1)} %get-tuple-element.21), channel_id=2, replica_groups=mesh['row'=16,'col'=16] {'row'}, dimensions={0}, use_global_device_ids=true | all-gather | bytes 136 | tf_op jit(solution)/shard_map/all_gather | solution.py:16
  208.4 0.6 fusion.27
  210.9 0.0 copy-done.1
  210.9 0.7 dynamic-slice
  211.6 0.8 dynamic-update-slice
  212.4 0.8 dynamic-update-slice.1
  213.2 0.8 dynamic-update-slice.2
  214.0 0.8 dynamic-update-slice.3
  214.8 11.2 %all-reduce.4 = (s32[16]{0:T(128)S(1)}, s32[16]{0:T(128)S(1)}, s32[16]{0:T(128)S(1)}, s32[16]{0:T(128)S(1)}) all-reduce(s32[16]{0:T(128)S(1)} %dynamic-update-slice.3, s32[16]{0:T(128)S(1)} %dynamic-update-slice.2, s32[16]{0:T(128)S(1)} %dynamic-update-slice.1, s32[16]{0:T(128)S(1)} %dynamic-update-slice), channel_id=1, replica_groups=mesh['row'=16,'col'=16] {'row'}, use_global_device_ids=true, to_apply=%add.3 | all-reduce | flops 64 | bytes 512
  225.9 0.7 reduce_sum.120
  227.9 41.4 %all-gather.2 = s32[16,1,2]{2,1,0:T(1,128)S(1)} all-gather(s32[1,1,2]{2,1,0:T(1,128)S(1)} %get-tuple-element.22), channel_id=4, replica_groups=mesh['row'=16,'col'=16] {'row'}, dimensions={0}, use_global_device_ids=true | all-gather | bytes 136 | tf_op jit(solution)/shard_map/all_gather | solution.py:16
  269.4 0.7 fusion.26
  270.7 0.6 reduce_sum.123
  273.1 35.7 %all-gather.4 = s32[16,1,2]{2,1,0:T(1,128)S(1)} all-gather(s32[1,1,2]{2,1,0:T(1,128)S(1)} %get-tuple-element.24), channel_id=6, replica_groups=mesh['row'=16,'col'=16] {'row'}, dimensions={0}, use_global_device_ids=true | all-gather | bytes 136 | tf_op jit(solution)/shard_map/all_gather | solution.py:16
  308.8 0.6 fusion.25
  309.9 0.6 reduce_sum.126
  312.4 37.7 %all-gather.6 = s32[16,1,2]{2,1,0:T(1,128)S(1)} all-gather(s32[1,1,2]{2,1,0:T(1,128)S(1)} %get-tuple-element.23), channel_id=8, replica_groups=mesh['row'=16,'col'=16] {'row'}, dimensions={0}, use_global_device_ids=true | all-gather | bytes 136 | tf_op jit(solution)/shard_map/all_gather | solution.py:16
  350.2 0.6 fusion.24
  351.4 0.6 reduce_sum.129
  353.9 0.0 all-gather.13.cloned.1.call-done
  353.9 2.9 reduce_sum.122
  356.8 0.0 all-gather.15.cloned.1.call-done
  356.8 2.9 reduce_sum.125
  359.7 78.8 %all-gather.17.cloned.1.call-done = bf16[16,1,2,256,256]{4,3,2,1,0:T(8,128)(2,1)} async-done(((bf16[1,1,2,256,256]{4,3,2,1,0:T(8,128)(2,1)}), bf16[16,1,2,256,256]{4,3,2,1,0:T(8,128)(2,1)}) %all-gather.17.cloned.1.call-update) | async-done | bytes 4194320 | tf_op jit(solution)/shard_map/all_gather | solution.py:16
  438.5 2.9 reduce_sum.128
  441.4 96.0 %all-gather.19.cloned.1.call-done = bf16[16,1,2,256,256]{4,3,2,1,0:T(8,128)(2,1)} async-done(((bf16[1,1,2,256,256]{4,3,2,1,0:T(8,128)(2,1)}), bf16[16,1,2,256,256]{4,3,2,1,0:T(8,128)(2,1)}) %all-gather.19.cloned.1.call-update) | async-done | bytes 4194320 | tf_op jit(solution)/shard_map/all_gather | solution.py:16
  537.3 2.9 reduce_sum.131
  540.2 2.0 convolution_select_fusion.6
  542.2 2.0 convolution_select_fusion.4
  544.3 2.1 fusion
  546.4 2.1 fusion.2
  548.5 2.0 convolution_select_fusion.2
  550.6 2.1 fusion.4
  552.7 0.0 collective-permute-done.2
  552.8 2.0 convolution_select_fusion
  554.8 3.4 fusion.7
  (9 shorter events, 0.2 us)
Async XLA Ops:
  6.5 347.4 %all-gather.13.cloned.1.call-start = ((), (), s32[]{:S(2)}) async-start(), calls=%async_computation | async-start | bytes 4456448 | tf_op jit(solution)/shard_map/all_gather | solution.py:16
  12.5 344.3 %all-gather.15.cloned.1.call-start = ((), (), s32[]{:S(2)}) async-start(), calls=%async_computation.1 | async-start | bytes 4456448 | tf_op jit(solution)/shard_map/all_gather | solution.py:16
  13.3 425.2 %all-gather.17.cloned.1.call-start = ((), (), s32[]{:S(2)}) async-start(), calls=%async_computation.2 | async-start | bytes 4456448 | tf_op jit(solution)/shard_map/all_gather | solution.py:16
  14.0 523.3 %all-gather.19.cloned.1.call-start = ((), (), s32[]{:S(2)}) async-start(), calls=%async_computation.3 | async-start | bytes 4456448 | tf_op jit(solution)/shard_map/all_gather | solution.py:16
  27.2 137.5 %copy-start = (s32[1,1,2]{2,1,0:T(1,128)S(1)}, s32[1,1,2]{2,1,0:T(1,128)}, u32[]{:S(2)}) copy-start(s32[1,1,2]{2,1,0:T(1,128)} %param.9) | copy-start | bytes 28
  27.2 183.7 %copy-start.1 = (u32[256]{0:T(256)S(1)}, u32[256]{0:T(256)}, u32[]{:S(2)}) copy-start(u32[256]{0:T(256)} %constant.57) | copy-start | bytes 3076
  35.3 54.9 %collective-permute-start = (bf16[3072,768]{0,1:T(8,128)(2,1)}, bf16[3072,768]{0,1:T(8,128)(2,1)}, u32[]{:S(2)}, u32[]{:S(2)}) collective-permute-start(bf16[3072,768]{0,1:T(8,128)(2,1)} %mul.61), channel_id=1, source_target_pairs={{0,1},{1,2},{2,3},{3,4},{4,5},{5,6},{6,7},{7,8},{8,9},{9,10},{10,1... | collective-permute-start | bytes 14155784 | tf_op jit(solution)/shard_map/ppermute | solution.py:11
  90.1 54.9 %collective-permute-start.1 = (bf16[3072,768]{0,1:T(8,128)(2,1)}, bf16[3072,768]{0,1:T(8,128)(2,1)}, u32[]{:S(2)}, u32[]{:S(2)}) collective-permute-start(bf16[3072,768]{0,1:T(8,128)(2,1)} %collective-permute-done), channel_id=1, source_target_pairs={{0,1},{1,2},{2,3},{3,4},{4,5},{5,6},{6,7},{7,8},{8,9},{9,10},{10,1... | collective-permute-start | bytes 14155784 | tf_op jit(solution)/shard_map/ppermute | solution.py:11
  145.0 407.7 %collective-permute-start.2 = (bf16[3072,768]{0,1:T(8,128)(2,1)}, bf16[3072,768]{0,1:T(8,128)(2,1)}, u32[]{:S(2)}, u32[]{:S(2)}) collective-permute-start(bf16[3072,768]{0,1:T(8,128)(2,1)} %collective-permute-done.1), channel_id=1, source_target_pairs={{0,1},{1,2},{2,3},{3,4},{4,5},{5,6},{6,7},{7,8},{8,9},{9,10},{10,1... | collective-permute-start | bytes 14155784 | tf_op jit(solution)/shard_map/ppermute | solution.py:11
Sparse Core Ops, SparseCore 0:
  12.6 114.2 all-gather.12
  129.5 210.0 all-gather.14
  342.2 96.2 all-gather.16
  440.9 96.3 all-gather.18
